TPU v7x, 512 devices: a whole 4x4x16 slice. The times are simulated.
512 devices in a mesh: clusters: 32 (over z, core), group: 16 (over x, y).
Axes of the slice: x: 4, y: 4, z: 16, core: 2. Of those that a mesh axis runs over, the one named last changes fastest.
Arguments:
- embeddings: bfloat16 [262144, 1024], P(('clusters', 'group')), may hold values from -20 to 20
- new_label: int32 [262144], P(('clusters', 'group')), may hold values from 0 to 31, as said below
- dest_member: int32 [262144], P(('clusters', 'group')), may hold values from 0 to 15, as said below
- seed_index: int32 [32, 512], P('clusters'), may hold values from 0 to 8191, as said below
- kappa: float32 [32], P('clusters'), may hold values from 8 to 400
Outputs:
- centroids: bfloat16 [16384, 1024], P('clusters')
- row_score: float32 [524288], P(('clusters', 'group'))
Inputs may be any that keep to these rules, and one draw needn't show every extreme that they name: `new_label`: each device sends between 192 and 320 of its rows to devices of other coarse clusters, at most 1 to any one device; in every draw one device receives exactly 1 row from every device of the other clusters, and every device sends exactly 1 row to some device. Rows whose label is their own device's cluster stay. `dest_member`: A row whose new_label is its own device's cluster has its own device's index along group here. `seed_index`: the 512 entries of cluster c are distinct positions m * 512 + s among the rows held before the move by cluster c's devices (m along group, s the row on that device), each naming a row whose new_label is c.
All inputs are finite; a program needn't handle non-finite values.
Results may differ from a plain program's by a relative error of at most 0.02.
The roundings to bfloat16 on the way count: a program that leaves them out, or rounds other values in their place, can miss the bound.
Values may be sent and summed in bfloat16 or wider, within the bound.
A program may use at most 64 MiB of HBM per device.

v0:
```python
import jax
import jax.numpy as jnp
from jax import lax
from jax.sharding import PartitionSpec as P

ITERS = 2
EPSILON = 1e-06


def unit_rows(embedded):
    values = embedded.astype(jnp.float32)
    scale = lax.rsqrt(jnp.sum(values * values, axis=-1, keepdims=True) + EPSILON)
    return (values * scale).astype(jnp.bfloat16)


def expectation(normed, alive, centres, concentration):
    scores = concentration * jnp.einsum(
        "sd,kd->sk", normed, centres, preferred_element_type=jnp.float32
    )
    largest = jnp.max(scores, axis=-1, keepdims=True)
    powered = jnp.exp(scores - largest)
    summed = jnp.sum(powered, axis=-1, keepdims=True)
    weights = (powered / summed * alive[:, None]).astype(jnp.bfloat16)
    log_norm = (largest[:, 0] + jnp.log(summed[:, 0])) * alive
    return (weights, log_norm)


def normalise(summed):
    length = jnp.sqrt(jnp.sum(summed * summed, axis=-1, keepdims=True))
    return (summed / jnp.maximum(length, 1.0)).astype(jnp.bfloat16)


def outgoing_rows(normed, moving, target, capacity, device_count):
    row_count = normed.shape[0]
    positions = jnp.arange(row_count, dtype=jnp.int32)
    matches = (
        (target[:, None] == target[None, :])
        & (positions[None, :] < positions[:, None])
        & moving[None, :]
    )
    earlier = jnp.sum(matches, axis=1)
    slot_index = jnp.where(moving, target * capacity + earlier, device_count * capacity)
    source_row = (
        jnp.full((device_count * capacity,), row_count, jnp.int32)
        .at[slot_index]
        .set(positions, mode="drop")
    )
    padded = jnp.concatenate([normed, jnp.zeros((1, normed.shape[1]), jnp.bfloat16)], axis=0)
    return (padded[source_row], (source_row < row_count).astype(jnp.bfloat16))


def shards(embeddings, new_label, dest_member, seed_index, kappa):
    row_count, feature_width = embeddings.shape
    cluster_count = lax.axis_size("clusters")
    member_count = lax.axis_size("group")
    device_count = cluster_count * member_count
    own_cluster = lax.axis_index("clusters")
    own_member = lax.axis_index("group")
    movers_most = row_count * 5 // 8
    other_devices = (cluster_count - 1) * member_count
    capacity = (movers_most + other_devices - 1) // other_devices
    normed = unit_rows(embeddings)
    moving = new_label != own_cluster
    target = new_label * member_count + dest_member
    leaving, filled = outgoing_rows(normed, moving, target, capacity, device_count)
    leaving = leaving.reshape(cluster_count, member_count, capacity, feature_width)
    filled = filled.reshape(cluster_count, member_count, capacity)
    arrived, occupied = (
        lax.all_to_all(
            lax.all_to_all(leaving, "clusters", split_axis=0, concat_axis=0, tiled=True),
            "group",
            split_axis=1,
            concat_axis=1,
            tiled=True,
        ),
        lax.all_to_all(
            lax.all_to_all(filled, "clusters", split_axis=0, concat_axis=0, tiled=True),
            "group",
            split_axis=1,
            concat_axis=1,
            tiled=True,
        ),
    )
    seed_rows = seed_index.reshape(-1)
    local_pos = seed_rows - own_member * row_count
    held_here = (local_pos >= 0) & (local_pos < row_count)
    chosen = jnp.where(
        held_here[:, None],
        normed[jnp.clip(local_pos, 0, row_count - 1)],
        jnp.zeros((), jnp.bfloat16),
    )
    centres = lax.psum(chosen.astype(jnp.float32).astype(jnp.bfloat16), "group")
    concentration = kappa[0]
    incoming = arrived.reshape(-1, feature_width)
    alive_in = occupied.reshape(-1).astype(jnp.float32)
    alive_own = jnp.where(moving, 0.0, 1.0).astype(jnp.float32)
    norm_own = alive_own
    norm_in = alive_in
    for iteration in range(ITERS):
        weights_own, norm_own = expectation(normed, alive_own, centres, concentration)
        weights_in, norm_in = expectation(incoming, alive_in, centres, concentration)
        partial_value = jnp.einsum(
            "sk,sd->kd", weights_own, normed, preferred_element_type=jnp.float32
        )
        partial_value = partial_value + jnp.einsum(
            "sk,sd->kd", weights_in, incoming, preferred_element_type=jnp.float32
        )
        centres = normalise(
            lax.psum(partial_value.astype(jnp.bfloat16), "group").astype(jnp.float32)
        )
    return (centres, jnp.concatenate([norm_own, norm_in]))


def solution(mesh):
    return jax.shard_map(
        shards,
        mesh=mesh,
        in_specs=(
            P(("clusters", "group"), None),
            P(("clusters", "group")),
            P(("clusters", "group")),
            P("clusters", None),
            P("clusters"),
        ),
        out_specs=(P("clusters", None), P(("clusters", "group"))),
        check_vma=False,
    )
```

profile of v0, /device:TPU:32, one launch (start us, length us, event | category | flops | bytes accessed | tf_op | source)
XLA Modules:
  0.0 431.6 jit_solution(14022457909516345308)
XLA Ops:
  7.2 0.7 multiply_add_fusion
  7.9 0.7 broadcast_select_fusion.1
  8.6 0.3 convert_reduce_fusion
  8.8 2.4 scatter_custom_fusion
  11.3 0.7 reshape.128
  12.0 15.4 %all-to-all-start.2 = ((bf16[32,16,1]{1,2,0:T(2,128)(2,1)}), bf16[32,16,1]{1,2,0:T(2,128)(2,1)S(1)}, u32[]{:S(2)}, u32[]{:S(2)}) async-start(bf16[32,16,1]{1,2,0:T(2,128)(2,1)} %reshape.128), calls=%async_computation.2 | async-start | bytes 32768 | tf_op jit(solution)/shard_map/all_to_all | solution.py:77
  27.4 1.5 fusion
  28.9 1.5 fusion.1
  30.4 0.1 concatenate.6
  30.5 2.8 gather_fusion.1
  33.2 0.0 copy-start.1
  33.2 5.3 %all-to-all-done.2 = bf16[32,16,1]{1,2,0:T(2,128)(2,1)S(1)} async-done(((bf16[32,16,1]{1,2,0:T(2,128)(2,1)}), bf16[32,16,1]{1,2,0:T(2,128)(2,1)S(1)}, u32[]{:S(2)}, u32[]{:S(2)}) %all-to-all-start.2) | async-done | bytes 1056 | tf_op jit(solution)/shard_map/all_to_all | solution.py:77
  38.6 7.0 %all-to-all-start = ((bf16[32,16,1,1024]{3,1,2,0:T(8,128)(2,1)}), bf16[32,16,1,1024]{3,1,2,0:T(8,128)(2,1)S(1)}, u32[]{:S(2)}, u32[]{:S(2)}) async-start(bf16[32,16,1,1024]{3,1,2,0:T(8,128)(2,1)} %bitcast.4), calls=%async_computation | async-start | bytes 2097152 | tf_op jit(solution)/shard_map/all_to_all | solution.py:70
  45.6 0.0 all-reduce.5.cloned.1.call-start
  45.6 0.0 copy-done.1
  45.7 2.1 gather_fusion
  47.8 1.1 broadcast_select_fusion
  48.9 0.0 all-reduce.5.cloned.1.call-update
  48.9 0.7 copy.28
  49.6 50.1 %all-to-all-done = bf16[32,16,1,1024]{3,1,2,0:T(8,128)(2,1)S(1)} async-done(((bf16[32,16,1,1024]{3,1,2,0:T(8,128)(2,1)}), bf16[32,16,1,1024]{3,1,2,0:T(8,128)(2,1)S(1)}, u32[]{:S(2)}, u32[]{:S(2)}) %all-to-all-start) | async-done | bytes 1048608 | tf_op jit(solution)/shard_map/all_to_all | solution.py:70
  99.7 7.0 %all-to-all-start.3 = ((bf16[32,16,1]{0,2,1:T(2,128)(2,1)}), bf16[32,16,1]{0,2,1:T(2,128)(2,1)S(1)}, u32[]{:S(2)}, u32[]{:S(2)}) async-start(bf16[32,16,1]{0,2,1:T(2,128)(2,1)} %copy.28), calls=%async_computation.3 | async-start | bytes 16384 | tf_op jit(solution)/shard_map/all_to_all | solution.py:76
  107.4 1.6 copy.25
  109.0 5.4 %all-to-all-done.3 = bf16[32,16,1]{0,2,1:T(2,128)(2,1)S(1)} async-done(((bf16[32,16,1]{0,2,1:T(2,128)(2,1)}), bf16[32,16,1]{0,2,1:T(2,128)(2,1)S(1)}, u32[]{:S(2)}, u32[]{:S(2)}) %all-to-all-start.3) | async-done | bytes 1056 | tf_op jit(solution)/shard_map/all_to_all | solution.py:76
  114.3 3.7 all-to-all-start.1
  118.0 0.0 all-reduce.7.cloned.1.call-start
  118.1 0.1 copy.30
  118.1 0.1 reshape.101
  118.2 51.1 %all-reduce.5.cloned.1.call-done = bf16[512,1024]{1,0:T(8,128)(2,1)} async-done(((bf16[512,1024]{1,0:T(8,128)(2,1)}), bf16[512,1024]{1,0:T(8,128)(2,1)}) %all-reduce.5.cloned.1.call-update) | async-done | bytes 1048592 | tf_op jit(solution)/shard_map/psum | solution.py:92
  169.3 2.0 fusion.30
  171.3 0.2 fusion.8
  171.5 2.1 fusion.12
  173.6 0.0 all-to-all-done.1
  173.6 0.0 copy-start.2
  173.6 0.6 copy.26
  174.2 0.6 copy-done.2
  174.8 0.0 copy-start.3
  174.8 0.8 fusion.31
  175.6 0.2 fusion.9
  175.8 0.6 copy-done.3
  176.4 1.7 add_convert_fusion.1
  178.1 0.0 all-reduce.7.cloned.1.call-update
  178.1 0.2 all-reduce.9.cloned.1.call-start
  178.4 117.4 %all-reduce.7.cloned.1.call-done = bf16[512,1024]{1,0:T(8,128)(2,1)} async-done(((bf16[512,1024]{1,0:T(8,128)(2,1)}), bf16[512,1024]{1,0:T(8,128)(2,1)}) %all-reduce.7.cloned.1.call-update) | async-done | bytes 1048592 | tf_op jit(solution)/shard_map/psum | solution.py:109
  295.7 1.5 fusion.2
  297.2 2.0 fusion.32
  299.2 0.2 fusion.10
  299.4 0.0 copy-start
  299.4 0.7 fusion.13
  300.2 0.5 copy-done
  300.7 0.8 fusion.33
  301.5 0.2 fusion.11
  301.7 1.7 add_convert_fusion
  303.4 0.0 all-reduce.9.cloned.1.call-update
  303.4 0.6 pad_maximum_fusion
  304.0 117.0 %all-reduce.9.cloned.1.call-done = bf16[512,1024]{1,0:T(8,128)(2,1)} async-done(((bf16[512,1024]{1,0:T(8,128)(2,1)}), bf16[512,1024]{1,0:T(8,128)(2,1)}) %all-reduce.9.cloned.1.call-update) | async-done | bytes 1048592 | tf_op jit(solution)/shard_map/psum | solution.py:109
  421.0 1.5 fusion.4
  422.5 2.5 fusion.5
  (13 shorter events, 0.1 us)
Async XLA Ops:
  12.0 26.6 %all-to-all-start.2 = ((bf16[32,16,1]{1,2,0:T(2,128)(2,1)}), bf16[32,16,1]{1,2,0:T(2,128)(2,1)S(1)}, u32[]{:S(2)}, u32[]{:S(2)}) async-start(bf16[32,16,1]{1,2,0:T(2,128)(2,1)} %reshape.128), calls=%async_computation.2 | async-start | bytes 32768 | tf_op jit(solution)/shard_map/all_to_all | solution.py:77
  33.2 12.4 %copy-start.1 = (s32[1,512]{1,0:T(1,128)S(1)}, s32[1,512]{1,0:T(1,128)}, u32[]{:S(2)}) copy-start(s32[1,512]{1,0:T(1,128)} %param.8) | copy-start | bytes 6148
  38.6 61.1 %all-to-all-start = ((bf16[32,16,1,1024]{3,1,2,0:T(8,128)(2,1)}), bf16[32,16,1,1024]{3,1,2,0:T(8,128)(2,1)S(1)}, u32[]{:S(2)}, u32[]{:S(2)}) async-start(bf16[32,16,1,1024]{3,1,2,0:T(8,128)(2,1)} %bitcast.4), calls=%async_computation | async-start | bytes 2097152 | tf_op jit(solution)/shard_map/all_to_all | solution.py:70
  45.6 123.8 %all-reduce.5.cloned.1.call-start = ((), (), s32[]{:S(2)}) async-start(), calls=%async_computation.4 | async-start | bytes 2097152 | tf_op jit(solution)/shard_map/psum | solution.py:92
  99.7 14.6 %all-to-all-start.3 = ((bf16[32,16,1]{0,2,1:T(2,128)(2,1)}), bf16[32,16,1]{0,2,1:T(2,128)(2,1)S(1)}, u32[]{:S(2)}, u32[]{:S(2)}) async-start(bf16[32,16,1]{0,2,1:T(2,128)(2,1)} %copy.28), calls=%async_computation.3 | async-start | bytes 16384 | tf_op jit(solution)/shard_map/all_to_all | solution.py:76
  114.3 59.2 %all-to-all-start.1 = ((bf16[32,16,1,1024]{3,0,2,1:T(8,128)(2,1)}), bf16[32,16,1,1024]{3,0,2,1:T(8,128)(2,1)S(1)}, u32[]{:S(2)}, u32[]{:S(2)}) async-start(bf16[32,16,1,1024]{3,0,2,1:T(8,128)(2,1)} %copy.25), calls=%async_computation.1 | async-start | bytes 2097152 | tf_op jit(solution)/shard_map/all_to_all | solution.py:69
  118.0 177.7 %all-reduce.7.cloned.1.call-start = ((), (), s32[]{:S(2)}) async-start(), calls=%async_computation.5 | async-start | bytes 2097152 | tf_op jit(solution)/shard_map/psum | solution.py:109
  173.6 1.2 copy-start.2
  174.8 1.6 copy-start.3
  178.1 242.9 %all-reduce.9.cloned.1.call-start = ((), (), s32[]{:S(2)}) async-start(), calls=%async_computation.6 | async-start | bytes 2097152 | tf_op jit(solution)/shard_map/psum | solution.py:109
  299.4 1.2 copy-start
Sparse Core Ops, SparseCore 0:
  50.2 119.0 all-reduce.4
  178.3 117.4 all-reduce.6
  303.5 117.4 all-reduce.8
where the time goes:
time: 432 us
  waiting for transfers between devices  346 us (80%)
  starting transfers between devices  33.4 us (8%)
  between operations  14.6 us (3%)
  other arithmetic  12.8 us (3%)
  local copies, waits for them, and re-layouts  12.8 us (3%)
  matrix products  11.7 us (3%)
    psum x2, waiting for transfers between devices, shards(): lax.psum(partial_value.astype(jnp.bfloat16), 'group').astype(jnp.float32)  234 us
    psum x1, waiting for transfers between devices, shards(): centres = lax.psum(chosen.astype(jnp.float32).astype(jnp.bfloat16), 'group')  51.1 us
    all_to_all x1, waiting for transfers between devices, shards(): lax.all_to_all(leaving, 'clusters', split_axis=0, concat_axis=0, tiled=True)  50.1 us
    all_to_all x1, starting transfers between devices, shards(): lax.all_to_all(filled, 'clusters', split_axis=0, concat_axis=0, tiled=True)  15.4 us
  transfers between devices with their start and end apart: 7, of which 6 were waited for; matrix products, arithmetic and copies ran while one was open for 4% of the time, Pallas kernels for 0%

commit v1 on v0

--- a/solution.py
+++ b/solution.py
@@ -5,6 +5,13 @@
 
 ITERS = 2
 EPSILON = 1e-06
+
+
+def swap_blocks(x, axis, split, join):
+    size = lax.axis_size(axis)
+    blocks = jnp.stack(jnp.split(x, size, axis=split), axis=0)
+    blocks = lax.all_to_all(blocks, axis, split_axis=0, concat_axis=0)
+    return jnp.concatenate(blocks, axis=join)
 
 
 def unit_rows(embedded):
@@ -66,12 +73,11 @@
     leaving = leaving.reshape(cluster_count, member_count, capacity, feature_width)
     filled = filled.reshape(cluster_count, member_count, capacity)
     arrived, occupied = (
-        lax.all_to_all(
+        swap_blocks(
             lax.all_to_all(leaving, "clusters", split_axis=0, concat_axis=0, tiled=True),
             "group",
-            split_axis=1,
-            concat_axis=1,
-            tiled=True,
+            1,
+            1,
         ),
         lax.all_to_all(
             lax.all_to_all(filled, "clusters", split_axis=0, concat_axis=0, tiled=True),

time: 432 us -> 435 us (level)
  waiting for transfers between devices: 346 us -> 334 us
  local copies, waits for them, and re-layouts: 12.8 us -> 23.8 us
    unnamed x8 -> x23, local copies, waits for them, and re-layouts: 1.79 us -> 11.4 us
    psum x1, waiting for transfers between devices: 51.1 us -> 45 us  [shards(): centres = lax.psum(chosen.astype(jnp.float32).astype(jnp.bfloat16), 'group')]
    all_to_all x1, waiting for transfers between devices: 5.38 us -> 0.01 us  [shards(): lax.all_to_all(lax.all_to_all(filled, 'clusters', split_axis=0, concat_ax...]
  transfers between devices with their start and end apart: 7 -> 7, of which waited for: 6 -> 5; matrix products, arithmetic and copies ran while one was open for 4% -> 6% of each run, Pallas kernels for 0% -> 0%
where the time goes in v1:
time: 435 us; the launch traced here: 434 us
  waiting for transfers between devices  334 us (77%)
  starting transfers between devices  36.9 us (8%)
  local copies, waits for them, and re-layouts  23.8 us (5%)
  between operations  14.6 us (3%)
  other arithmetic  12.8 us (3%)
  matrix products  11.8 us (3%)
    psum x2, waiting for transfers between devices, shards(): lax.psum(partial_value.astype(jnp.bfloat16), 'group').astype(jnp.float32)  234 us
    all_to_all x1, waiting for transfers between devices, shards(): lax.all_to_all(leaving, 'clusters', split_axis=0, concat_axis=0, tiled=True)  49.5 us
    psum x1, waiting for transfers between devices, shards(): centres = lax.psum(chosen.astype(jnp.float32).astype(jnp.bfloat16), 'group')  45 us
    all_to_all x1, starting transfers between devices, shards(): lax.all_to_all(filled, 'clusters', split_axis=0, concat_axis=0, tiled=True)  15.4 us
    unnamed x23, local copies, waits for them, and re-layouts  11.4 us
  transfers between devices with their start and end apart: 7, of which 5 were waited for; matrix products, arithmetic and copies ran while one was open for 6% of the time, Pallas kernels for 0%

profile of v1, /device:TPU:32, one launch (start us, length us, event | category | flops | bytes accessed | tf_op | source)
XLA Modules:
  0.0 434.0 jit_solution(15847107451881946460)
XLA Ops:
  7.2 0.7 broadcast_select_fusion.1
  7.9 0.7 multiply_add_fusion
  8.6 0.3 convert_reduce_fusion
  8.8 2.4 scatter_custom_fusion
  11.3 0.7 reshape.128
  12.0 15.4 %all-to-all-start.2 = ((bf16[32,16,1]{1,2,0:T(2,128)(2,1)}), bf16[32,16,1]{1,2,0:T(2,128)(2,1)S(1)}, u32[]{:S(2)}, u32[]{:S(2)}) async-start(bf16[32,16,1]{1,2,0:T(2,128)(2,1)} %reshape.128), calls=%async_computation.2 | async-start | bytes 32768 | tf_op jit(solution)/shard_map/all_to_all | solution.py:83
  27.4 1.5 fusion
  28.9 1.5 fusion.1
  30.4 0.1 concatenate.6
  30.5 2.8 gather_fusion.1
  33.2 5.3 %all-to-all-done.2 = bf16[32,16,1]{1,2,0:T(2,128)(2,1)S(1)} async-done(((bf16[32,16,1]{1,2,0:T(2,128)(2,1)}), bf16[32,16,1]{1,2,0:T(2,128)(2,1)S(1)}, u32[]{:S(2)}, u32[]{:S(2)}) %all-to-all-start.2) | async-done | bytes 1056 | tf_op jit(solution)/shard_map/all_to_all | solution.py:83
  38.6 7.0 %all-to-all-start = ((bf16[32,16,1,1024]{3,1,2,0:T(8,128)(2,1)}), bf16[32,16,1,1024]{3,1,2,0:T(8,128)(2,1)S(1)}, u32[]{:S(2)}, u32[]{:S(2)}) async-start(bf16[32,16,1,1024]{3,1,2,0:T(8,128)(2,1)} %bitcast.4), calls=%async_computation | async-start | bytes 2097152 | tf_op jit(solution)/shard_map/all_to_all | solution.py:77
  45.6 0.0 all-reduce.5.cloned.1.call-start
  45.7 2.1 gather_fusion
  47.8 1.1 broadcast_select_fusion
  48.9 0.0 all-reduce.5.cloned.1.call-update
  49.5 0.7 copy.106
  50.2 49.5 %all-to-all-done = bf16[32,16,1,1024]{3,1,2,0:T(8,128)(2,1)S(1)} async-done(((bf16[32,16,1,1024]{3,1,2,0:T(8,128)(2,1)}), bf16[32,16,1,1024]{3,1,2,0:T(8,128)(2,1)S(1)}, u32[]{:S(2)}, u32[]{:S(2)}) %all-to-all-start) | async-done | bytes 1048608 | tf_op jit(solution)/shard_map/all_to_all | solution.py:77
  99.7 7.0 %all-to-all-start.3 = ((bf16[32,16,1]{0,2,1:T(2,128)(2,1)}), bf16[32,16,1]{0,2,1:T(2,128)(2,1)S(1)}, u32[]{:S(2)}, u32[]{:S(2)}) async-start(bf16[32,16,1]{0,2,1:T(2,128)(2,1)} %copy.106), calls=%async_computation.3 | async-start | bytes 16384 | tf_op jit(solution)/shard_map/all_to_all | solution.py:82
  106.7 2.3 fusion.46
  109.0 0.6 fusion.41
  109.7 0.6 fusion.40
  110.3 0.6 fusion.39
  111.0 0.6 fusion.38
  111.6 0.6 fusion.37
  112.3 0.6 fusion.36
  112.9 0.6 fusion.35
  113.5 0.6 fusion.34
  114.2 0.6 fusion.33
  114.8 0.6 fusion.32
  115.4 0.7 fusion.31
  116.1 0.6 fusion.30
  116.7 0.6 fusion.29
  117.4 0.6 fusion.28
  118.0 0.6 fusion.27
  118.7 0.6 fusion.26
  119.3 7.2 %all-to-all-start.1 = ((bf16[16,32,1,1,1024]{4,1,3,2,0:T(8,128)(2,1)}), bf16[16,32,1,1,1024]{4,1,3,2,0:T(8,128)(2,1)S(1)}, u32[]{:S(2)}, u32[]{:S(2)}) async-start(bf16[16,32,1,1,1024]{4,1,3,2,0:T(8,128)(2,1)} %fusion.26), calls=%async_computation.1 | async-start | bytes 2097152 | tf_op jit(solution)/shard_map/all_to_all | solution.py:13
  126.5 0.0 all-reduce.7.cloned.1.call-start
  126.6 0.1 copy.108
  126.7 0.1 reshape.101
  126.7 45.0 %all-reduce.5.cloned.1.call-done = bf16[512,1024]{1,0:T(8,128)(2,1)} async-done(((bf16[512,1024]{1,0:T(8,128)(2,1)}), bf16[512,1024]{1,0:T(8,128)(2,1)}) %all-reduce.5.cloned.1.call-update) | async-done | bytes 1048592 | tf_op jit(solution)/shard_map/psum | solution.py:98
  171.7 2.0 fusion.47
  173.7 0.2 fusion.8
  173.9 2.1 fusion.12
  176.0 0.6 copy.104
  176.6 0.6 copy-done.2
  177.2 0.8 fusion.48
  178.0 0.2 fusion.9
  178.2 0.6 copy-done.3
  178.8 1.7 add_convert_fusion.1
  180.5 0.2 all-reduce.9.cloned.1.call-start
  180.7 117.4 %all-reduce.7.cloned.1.call-done = bf16[512,1024]{1,0:T(8,128)(2,1)} async-done(((bf16[512,1024]{1,0:T(8,128)(2,1)}), bf16[512,1024]{1,0:T(8,128)(2,1)}) %all-reduce.7.cloned.1.call-update) | async-done | bytes 1048592 | tf_op jit(solution)/shard_map/psum | solution.py:115
  298.1 1.5 fusion.2
  299.6 2.0 fusion.49
  301.6 0.2 fusion.10
  301.8 0.7 fusion.13
  302.5 0.5 copy-done
  303.0 0.8 fusion.50
  303.8 0.2 fusion.11
  304.0 1.7 add_convert_fusion
  305.8 0.6 pad_maximum_fusion
  306.4 117.0 %all-reduce.9.cloned.1.call-done = bf16[512,1024]{1,0:T(8,128)(2,1)} async-done(((bf16[512,1024]{1,0:T(8,128)(2,1)}), bf16[512,1024]{1,0:T(8,128)(2,1)}) %all-reduce.9.cloned.1.call-update) | async-done | bytes 1048592 | tf_op jit(solution)/shard_map/psum | solution.py:115
  423.4 1.5 fusion.4
  424.9 2.5 fusion.5
  (22 shorter events, 0.2 us)
Async XLA Ops:
  12.0 26.6 %all-to-all-start.2 = ((bf16[32,16,1]{1,2,0:T(2,128)(2,1)}), bf16[32,16,1]{1,2,0:T(2,128)(2,1)S(1)}, u32[]{:S(2)}, u32[]{:S(2)}) async-start(bf16[32,16,1]{1,2,0:T(2,128)(2,1)} %reshape.128), calls=%async_computation.2 | async-start | bytes 32768 | tf_op jit(solution)/shard_map/all_to_all | solution.py:83
  33.2 12.4 %copy-start.1 = (s32[1,512]{1,0:T(1,128)S(1)}, s32[1,512]{1,0:T(1,128)}, u32[]{:S(2)}) copy-start(s32[1,512]{1,0:T(1,128)} %param.8) | copy-start | bytes 6148
  38.6 61.1 %all-to-all-start = ((bf16[32,16,1,1024]{3,1,2,0:T(8,128)(2,1)}), bf16[32,16,1,1024]{3,1,2,0:T(8,128)(2,1)S(1)}, u32[]{:S(2)}, u32[]{:S(2)}) async-start(bf16[32,16,1,1024]{3,1,2,0:T(8,128)(2,1)} %bitcast.4), calls=%async_computation | async-start | bytes 2097152 | tf_op jit(solution)/shard_map/all_to_all | solution.py:77
  45.6 126.1 %all-reduce.5.cloned.1.call-start = ((), (), s32[]{:S(2)}) async-start(), calls=%async_computation.4 | async-start | bytes 2097152 | tf_op jit(solution)/shard_map/psum | solution.py:98
  99.7 19.6 %all-to-all-start.3 = ((bf16[32,16,1]{0,2,1:T(2,128)(2,1)}), bf16[32,16,1]{0,2,1:T(2,128)(2,1)S(1)}, u32[]{:S(2)}, u32[]{:S(2)}) async-start(bf16[32,16,1]{0,2,1:T(2,128)(2,1)} %copy.106), calls=%async_computation.3 | async-start | bytes 16384 | tf_op jit(solution)/shard_map/all_to_all | solution.py:82
  119.3 56.7 %all-to-all-start.1 = ((bf16[16,32,1,1,1024]{4,1,3,2,0:T(8,128)(2,1)}), bf16[16,32,1,1,1024]{4,1,3,2,0:T(8,128)(2,1)S(1)}, u32[]{:S(2)}, u32[]{:S(2)}) async-start(bf16[16,32,1,1,1024]{4,1,3,2,0:T(8,128)(2,1)} %fusion.26), calls=%async_computation.1 | async-start | bytes 2097152 | tf_op jit(solution)/shard_map/all_to_all | solution.py:13
  126.5 171.6 %all-reduce.7.cloned.1.call-start = ((), (), s32[]{:S(2)}) async-start(), calls=%async_computation.5 | async-start | bytes 2097152 | tf_op jit(solution)/shard_map/psum | solution.py:115
  176.0 1.2 copy-start.2
  177.2 1.6 copy-start.3
  180.5 242.9 %all-reduce.9.cloned.1.call-start = ((), (), s32[]{:S(2)}) async-start(), calls=%async_computation.6 | async-start | bytes 2097152 | tf_op jit(solution)/shard_map/psum | solution.py:115
  301.8 1.2 copy-start
Sparse Core Ops, SparseCore 0:
  50.2 121.4 all-reduce.4
  180.6 117.4 all-reduce.6
  305.9 117.4 all-reduce.8
